TPU v7x, 32 devices: a whole 2x2x4 slice. The times are simulated.
32 devices in a mesh: groups: 2 (over x), corpus: 16 (over z, y, core).
Axes of the slice: x: 2, y: 2, z: 4, core: 2. Of those that a mesh axis runs over, the one named last changes fastest.
Arguments:
- queries: bfloat16 [1792, 32, 128], P(('groups', 'corpus')), parts along dimension 0, may hold values from -6 to 6
- passages: bfloat16 [4096, 128, 128], P(('groups', 'corpus')), parts along dimension 0, may hold values from -0.5 to 0.5
- lengths: int32 [4096], P(('groups', 'corpus')), parts along dimension 0, may hold values from 8 to 128
- candidates: int32 [32, 128], P(('groups', 'corpus')), parts along dimension 0, may hold values from 0 to 2047, as said below
Outputs:
- scores: float32 [1792, 128], P(('groups', 'corpus')), parts along dimension 0
- best_scores: float32 [1792, 100], P(('groups', 'corpus')), parts along dimension 0
There are 2 independent parts, one for each index of `groups`. A program takes and returns all parts, laid end to end along the dimension named above; each array names one. Nothing has to cross between parts.
Inputs may be any that keep to these rules, and one draw needn't show every extreme that they name: Row b lists the candidates of queries b * 56 to (b + 1) * 56 - 1. Passage p is held by owner p // 128. In every row at most 12 entries share an owner, and in every row some owner holds exactly 12 of them. Entries may repeat. `lengths`: rows of a tile at or past its length are padding.
All inputs are finite; a program needn't handle non-finite values.
Results may differ from a plain program's by a relative error of at most 0.0003.
Values may be sent and summed in bfloat16 or wider, within the bound.
A program may use at most 128 MiB of HBM per device.

v0:
```python
import math
import jax
import jax.numpy as jnp
from jax import lax
from jax.sharding import PartitionSpec as P

TOPK = 100


def maxsim_many(query_sets, tile_sets, per_device):
    similar = jnp.einsum(
        "srd,sgpd->srgp", query_sets, tile_sets, preferred_element_type=jnp.float32
    )
    nearest = jnp.max(similar, axis=3)
    shards_now = query_sets.shape[0]
    query_tok = query_sets.shape[1] // per_device
    return jnp.sum(
        nearest.reshape(shards_now, per_device, query_tok, nearest.shape[2]), axis=2
    ) / float(query_tok)


def fill_rows(tile_set, tile_len):
    inside = lax.broadcasted_iota(jnp.int32, tile_set.shape[:2], 1) < tile_len[:, None]
    return jnp.where(inside[:, :, None], tile_set, tile_set[:, :1, :])


def local(queries, passages, lengths, candidates):
    peers = lax.axis_size("corpus")
    per_owner, tile_rows, feature = passages.shape
    per_device, query_tok = (queries.shape[0], queries.shape[1])
    candidate_ids = candidates[0]
    number = candidate_ids.shape[0]
    capacity = max(2, 3 * number // (2 * peers))
    owner_of = candidate_ids // per_owner
    local_id = candidate_ids - owner_of * per_owner
    position = jnp.arange(number, dtype=jnp.int32)
    shared = (owner_of[:, None] == owner_of[None, :]) & (position[None, :] < position[:, None])
    rank_in = jnp.sum(shared.astype(jnp.int32), axis=1)
    slot_of = owner_of * capacity + rank_in
    matches = slot_of[None, :] == jnp.arange(peers * capacity, dtype=jnp.int32)[:, None]
    wanted = jnp.max(jnp.where(matches, local_id[None, :], -1), axis=1).reshape(peers, capacity)
    asked = lax.all_to_all(wanted, "corpus", split_axis=0, concat_axis=0, tiled=True)
    picked = jnp.maximum(asked.reshape(-1), 0)
    chosen = fill_rows(passages[picked], lengths[picked])
    by_scorer = chosen.reshape(peers, capacity, tile_rows, feature)
    stacked = queries.reshape(1, per_device * query_tok, feature)
    piece = lax.all_gather(stacked, "corpus", axis=0, tiled=True)
    shards_here = piece.shape[0]
    group_size = math.gcd(shards_here, 8)
    turns = shards_here // group_size
    query_groups = piece.reshape(turns, group_size, piece.shape[1], feature)
    tile_groups = by_scorer.reshape(turns, group_size, capacity, tile_rows, feature)
    fresh_scores = lax.map(
        lambda paired: maxsim_many(paired[0], paired[1], per_device), (query_groups, tile_groups)
    )
    fresh_scores = fresh_scores.reshape(shards_here, per_device, capacity)
    returned = lax.all_to_all(fresh_scores, "corpus", split_axis=0, concat_axis=0, tiled=True)
    spread = jnp.transpose(returned, (1, 0, 2)).reshape(per_device, peers * capacity)
    scores = jnp.take(spread, slot_of, axis=1)
    best_scores = lax.top_k(scores, TOPK)[0]
    return (scores, best_scores)


def solution(mesh):
    return jax.shard_map(
        local,
        mesh=mesh,
        in_specs=(
            P(("groups", "corpus"), None, None),
            P(("groups", "corpus"), None, None),
            P(("groups", "corpus")),
            P(("groups", "corpus"), None),
        ),
        out_specs=(P(("groups", "corpus"), None), P(("groups", "corpus"), None)),
        check_vma=False,
    )
```

profile of v0, /device:TPU:0, one launch (start us, length us, event | category | flops | bytes accessed | tf_op | source)
XLA Modules:
  0.0 137.0 jit_solution(5977993929277204286)
XLA Ops:
  7.2 0.7 all-gather.2.cloned.1.call-update
  7.9 0.7 subtract_bitcast_fusion
  9.6 0.7 all_to_all.9
  10.3 7.4 %all-to-all-start = ((s32[16,1,12]{2,1,0:T(1,128)}), s32[16,1,12]{2,1,0:T(1,128)S(1)}, u32[]{:S(2)}, u32[]{:S(2)}) async-start(s32[16,1,12]{2,1,0:T(1,128)} %bitcast.12), calls=%async_computation | async-start | bytes 16384 | tf_op jit(solution)/shard_map/all_to_all | solution.py:42
  17.7 0.7 fusion.6
  18.3 0.7 compare_and_fusion
  19.0 5.0 %all-to-all-done = s32[16,1,12]{2,1,0:T(1,128)S(1)} async-done(((s32[16,1,12]{2,1,0:T(1,128)}), s32[16,1,12]{2,1,0:T(1,128)S(1)}, u32[]{:S(2)}, u32[]{:S(2)}) %all-to-all-start) | async-done | bytes 800 | tf_op jit(solution)/shard_map/all_to_all | solution.py:42
  24.2 10.2 %gather_fusion.1 = bf16[192,128,128]{2,1,0:T(8,128)(2,1)} fusion(bf16[128,128,128]{2,1,0:T(8,128)(2,1)} %param.7, s32[1024]{0:T(1024)S(1)} %pad_clamp_fusion.1), kind=kCustom, calls=%fused_computation.1 | custom fusion | bytes 12583680 | tf_op jit(solution)/shard_map/gather | solution.py:44
  34.3 1.3 slice_reduce_fusion
  35.6 1.6 %gather_fusion = s32[192]{0:T(256)S(1)} fusion(s32[128]{0:T(128)S(1)} %copy-done, s32[1024]{0:T(1024)S(1)} %pad_clamp_fusion.1), kind=kCustom, calls=%fused_computation | custom fusion | bytes 2304 | tf_op jit(solution)/shard_map/gather | solution.py:44
  37.4 6.5 %broadcast_select_fusion = bf16[2,8,12,128,128]{4,3,2,1,0:T(8,128)(2,1)} fusion(bf16[2,8,12,128,128]{4,3,2,1,0:T(8,128)(2,1)} %bitcast.73, pred[2,8,12,128]{3,2,1,0:T(8,128)(4,1)S(1)} %iota_compare_fusion, bf16[2,8,12,128]{3,2,1,0:T(8,128)(2,1)S(1)} %broadcast_in_dim.64), kind=kLoop, calls=%fused_computation.10 | loop fusion | flops 3145728 | bytes 12656640 | tf_op jit(solution)/shard_map/jit(_where)/select_n | solution.py:24
  43.9 36.8 %all-gather.2.cloned.1.call-done = bf16[16,1792,128]{2,1,0:T(8,128)(2,1)} async-done(((bf16[1,1792,128]{2,1,0:T(8,128)(2,1)}), bf16[16,1792,128]{2,1,0:T(8,128)(2,1)}) %all-gather.2.cloned.1.call-update) | async-done | bytes 7340048 | tf_op jit(solution)/shard_map/all_gather | solution.py:47
  80.7 32.9 %while.10 = (s32[]{:T(128)}, f32[2,8,56,12]{2,1,0,3:T(8,128)S(1)}, bf16[2,8,1792,128]{3,2,1,0:T(8,128)(2,1)}, bf16[2,8,12,128,128]{4,3,2,1,0:T(8,128)(2,1)}, s32[]{:T(128)}, /*index=5*/f32[]{:T(128)}) while((s32[]{:T(128)}, f32[2,8,56,12]{2,1,0,3:T(8,128)S(1)}, bf16[2,8,1792,128]{3,2,1,0:T(8,128)(2,1)}, ...), condition=%wide.region_5.6_spmd, body=%wide.region_2.5_spmd.sunk | while | flops 5659164672 | bytes 11065421 | solution.py:53
  80.7 14.4 %convolution_reduce_fusion.2 = f32[8,1792,12]{1,2,0:T(8,128)S(1)} fusion(bf16[2,8,1792,128]{3,2,1,0:T(8,128)(2,1)} %get-tuple-element.87, s32[]{:T(128)} %get-tuple-element.79, bf16[2,8,12,128,128]{4,3,2,1,0:T(8,128)(2,1)} %get-tuple-element.88), kind=kOutput, calls=%fused_computation.3.clone.1 | convolution fusion | flops 5658992640 | bytes 7504896 | tf_op jit(solution)/shard_map/while/body/eval_jaxpr/srd,sgpd->srgp/dot_general | solution.py:11
  95.5 0.8 reshape.220
  96.4 0.8 reduce_sum.27
  97.2 14.4 %convolution_reduce_fusion.2 = f32[8,1792,12]{1,2,0:T(8,128)S(1)} fusion(bf16[2,8,1792,128]{3,2,1,0:T(8,128)(2,1)} %get-tuple-element.87, s32[]{:T(128)} %get-tuple-element.79, bf16[2,8,12,128,128]{4,3,2,1,0:T(8,128)(2,1)} %get-tuple-element.88), kind=kOutput, calls=%fused_computation.3.clone.1 | convolution fusion | flops 5658992640 | bytes 7504896 | tf_op jit(solution)/shard_map/while/body/eval_jaxpr/srd,sgpd->srgp/dot_general | solution.py:11
  112.0 0.8 reshape.220
  112.8 0.8 reduce_sum.27
  113.7 0.8 reshape.217
  114.5 3.5 %all-to-all-start.1 = ((f32[16,1,672]{2,1,0:T(1,128)}), f32[16,1,672]{2,1,0:T(1,128)S(1)}, u32[]{:S(2)}, u32[]{:S(2)}) async-start(f32[16,1,672]{2,1,0:T(1,128)} %reshape.217), calls=%async_computation.1 | async-start | bytes 98304 | tf_op jit(solution)/shard_map/all_to_all | solution.py:57
  118.0 6.7 %all-to-all-done.1 = f32[16,1,672]{2,1,0:T(1,128)S(1)} async-done(((f32[16,1,672]{2,1,0:T(1,128)}), f32[16,1,672]{2,1,0:T(1,128)S(1)}, u32[]{:S(2)}, u32[]{:S(2)}) %all-to-all-start.1) | async-done | bytes 43040 | tf_op jit(solution)/shard_map/all_to_all | solution.py:57
  125.2 0.8 reduce.6
  126.9 3.2 %top_k.9 = (f32[56,128]{1,0:T(8,128)}, s32[56,128]{1,0:T(8,128)}) sort(f32[56,128]{1,0:T(8,128)S(1)} %copy.27, s32[56,128]{1,0:T(8,128)S(1)} %iota.22), dimensions={1}, to_apply=%region_6.7 | sort | flops 93184 | bytes 114688 | tf_op jit(solution)/shard_map/top_k | solution.py:60
  (30 shorter events, 3.6 us)
Async XLA Ops:
  7.2 28.5 %copy-start = (s32[128]{0:T(128)S(1)}, s32[128]{0:T(128)}, u32[]{:S(2)}) copy-start(s32[128]{0:T(128)} %param.8) | copy-start | bytes 1540
  7.2 73.5 %all-gather.2.cloned.1.call-start = ((), (), s32[]{:S(2)}) async-start(), calls=%async_computation.2 | async-start | bytes 7798784 | tf_op jit(solution)/shard_map/all_gather | solution.py:47
  10.3 13.8 %all-to-all-start = ((s32[16,1,12]{2,1,0:T(1,128)}), s32[16,1,12]{2,1,0:T(1,128)S(1)}, u32[]{:S(2)}, u32[]{:S(2)}) async-start(s32[16,1,12]{2,1,0:T(1,128)} %bitcast.12), calls=%async_computation | async-start | bytes 16384 | tf_op jit(solution)/shard_map/all_to_all | solution.py:42
  114.5 10.2 %all-to-all-start.1 = ((f32[16,1,672]{2,1,0:T(1,128)}), f32[16,1,672]{2,1,0:T(1,128)S(1)}, u32[]{:S(2)}, u32[]{:S(2)}) async-start(f32[16,1,672]{2,1,0:T(1,128)} %reshape.217), calls=%async_computation.1 | async-start | bytes 98304 | tf_op jit(solution)/shard_map/all_to_all | solution.py:57
  126.9 3.2 %copy-start.1 = (f32[56,128]{1,0:T(8,128)}, f32[56,128]{1,0:T(8,128)S(1)}, u32[]{:S(2)}) copy-start(f32[56,128]{1,0:T(8,128)S(1)} %copy.27) | copy-start | bytes 86020
Sparse Core Ops, SparseCore 0:
  10.3 70.3 all-gather.1
where the time goes:
time: 137 us
  waiting for transfers between devices  49.2 us (36%)
  matrix products  28.8 us (21%)
  local copies, waits for them, and re-layouts  18.4 us (13%)
  other arithmetic  15.3 us (11%)
  between operations  14.2 us (10%)
  starting transfers between devices  10.9 us (8%)
    all_gather x1, waiting for transfers between devices, local(): piece = lax.all_gather(stacked, 'corpus', axis=0, tiled=True)  36.8 us
    dot_general x2, matrix products, maxsim_many(): jnp.einsum('srd,sgpd->srgp', query_sets, tile_sets, preferred_element_typ...  28.8 us
    gather x2, local copies, waits for them, and re-layouts, local(): chosen = fill_rows(passages[picked], lengths[picked])  11.7 us
    all_to_all x1, starting transfers between devices, local(): lax.all_to_all(wanted, 'corpus', split_axis=0, concat_axis=0, tiled=True)  7.41 us
    all_to_all x1, waiting for transfers between devices, local(): lax.all_to_all(fresh_scores, 'corpus', split_axis=0, concat_axis=0, tiled...  6.72 us
    select_n x1, other arithmetic, fill_rows(): return jnp.where(inside[:, :, None], tile_set, tile_set[:, :1, :])  6.55 us
    all_to_all x1, waiting for transfers between devices, local(): lax.all_to_all(wanted, 'corpus', split_axis=0, concat_axis=0, tiled=True)  5.01 us
    all_to_all x1, starting transfers between devices, local(): lax.all_to_all(fresh_scores, 'corpus', split_axis=0, concat_axis=0, tiled...  3.5 us
  transfers between devices with their start and end apart: 3, of which 3 were waited for; matrix products, arithmetic and copies ran while one was open for 17% of the time, Pallas kernels for 0%

commit v1 on v0

--- a/solution.py
+++ b/solution.py
@@ -44,7 +44,19 @@
     chosen = fill_rows(passages[picked], lengths[picked])
     by_scorer = chosen.reshape(peers, capacity, tile_rows, feature)
     stacked = queries.reshape(1, per_device * query_tok, feature)
-    piece = lax.all_gather(stacked, "corpus", axis=0, tiled=True)
+    n = lax.axis_size("corpus")
+    tray = [(t, (t + 1) % n) for t in range(n)]
+    by_rank = [(t, (t - 1) % n) for t in range(n)]
+    r1, u_next = ([stacked], [stacked])
+    for _ in range(n // 2):
+        arr_out = lax.ppermute(r1[-1], "corpus", tray)
+        r1.append(arr_out)
+    kk = 0
+    while kk < (n - 1) // 2:
+        u_next.append(lax.ppermute(u_next[-1], "corpus", by_rank))
+        kk = kk + 1
+    y_new = jnp.concatenate([*r1[::-1], *u_next[1:]], 0)
+    piece = jnp.roll(y_new, (lax.axis_index("corpus") - n // 2) * stacked.shape[0], 0)
     shards_here = piece.shape[0]
     group_size = math.gcd(shards_here, 8)
     turns = shards_here // group_size

time: 137 us -> 194 us (1.42)
  local copies, waits for them, and re-layouts: 18.4 us -> 59.3 us
  starting transfers between devices: 10.9 us -> 42.9 us
  between operations: 14.2 us -> 0.92 us
  waiting for transfers between devices: 49.2 us -> 46.8 us
    all_gather x1 -> x0, waiting for transfers between devices: 36.8 us -> none  [local(): piece = lax.all_gather(stacked, 'corpus', axis=0, tiled=True)]
    ppermute x0 -> x15, waiting for transfers between devices: none -> 34.5 us  [the longest x8 34.4 us: local(): arr_out = lax.ppermute(r1[-1], 'corpus', tray)]
    unnamed x7 -> x50, local copies, waits for them, and re-layouts: 0.95 us -> 34.2 us
    ppermute x0 -> x15, starting transfers between devices: none -> 32.5 us  [the longest x7 23.6 us: local(): u_next.append(lax.ppermute(u_next[-1], 'corpus', by_rank))]
    dynamic_slice x0 -> x1, local copies, waits for them, and re-layouts: none -> 6.73 us  [local(): jnp.roll(y_new, (lax.axis_index('corpus') - n // 2) * stacked.shape[0], 0)]
  transfers between devices with their start and end apart: 3 -> 17, of which waited for: 3 -> 7; matrix products, arithmetic and copies ran while one was open for 17% -> 20% of each run, Pallas kernels for 0% -> 0%
where the time goes in v1:
time: 194 us; the launch traced here: 193 us
  local copies, waits for them, and re-layouts  59.3 us (31%)
  waiting for transfers between devices  46.8 us (24%)
  starting transfers between devices  42.9 us (22%)
  matrix products  28.8 us (15%)
  other arithmetic  14.6 us (8%)
    ppermute x8, waiting for transfers between devices, local(): arr_out = lax.ppermute(r1[-1], 'corpus', tray)  34.4 us
    unnamed x50, local copies, waits for them, and re-layouts  34.2 us
    dot_general x2, matrix products, maxsim_many(): jnp.einsum('srd,sgpd->srgp', query_sets, tile_sets, preferred_element_typ...  28.8 us
    ppermute x7, starting transfers between devices, local(): u_next.append(lax.ppermute(u_next[-1], 'corpus', by_rank))  23.6 us
    gather x2, local copies, waits for them, and re-layouts, local(): chosen = fill_rows(passages[picked], lengths[picked])  11.8 us
    ppermute x8, starting transfers between devices, local(): arr_out = lax.ppermute(r1[-1], 'corpus', tray)  8.96 us
    all_to_all x1, starting transfers between devices, local(): lax.all_to_all(wanted, 'corpus', split_axis=0, concat_axis=0, tiled=True)  6.83 us
    dynamic_slice x1, local copies, waits for them, and re-layouts, local(): jnp.roll(y_new, (lax.axis_index('corpus') - n // 2) * stacked.shape[0], 0)  6.73 us
  transfers between devices with their start and end apart: 17, of which 7 were waited for; matrix products, arithmetic and copies ran while one was open for 20% of the time, Pallas kernels for 0%

profile of v1, /device:TPU:0, one launch (start us, length us, event | category | flops | bytes accessed | tf_op | source)
XLA Modules:
  0.0 193.4 jit_solution(15736280296141465445)
XLA Ops:
  1.2 11.4 %collective-permute-done = bf16[1,1792,128]{2,1,0:T(8,128)(2,1)S(1)} collective-permute-done((bf16[1,1792,128]{2,1,0:T(8,128)(2,1)}, bf16[1,1792,128]{2,1,0:T(8,128)(2,1)S(1)}, u32[]{:S(2)}, u32[]{:S(2)}) %collective-permute-start) | collective-permute-done | bytes 458784 | tf_op jit(solution)/shard_map/ppermute | solution.py:52
  12.6 4.4 %collective-permute-start.8 = (bf16[1,1792,128]{2,1,0:T(8,128)(2,1)}, bf16[1,1792,128]{2,1,0:T(8,128)(2,1)S(1)}, u32[]{:S(2)}, u32[]{:S(2)}) collective-permute-start(bf16[1,1792,128]{2,1,0:T(8,128)(2,1)} %bitcast.80), channel_id=1, source_target_pairs={{0,15},{1,0},{2,1},{3,2},{4,3},{5,4},{6,5},{7,6},{8,7},{9,8},{10,9... | collective-permute-start | bytes 1376264 | tf_op jit(solution)/shard_map/ppermute | solution.py:56
  17.0 6.3 %collective-permute-done.1 = bf16[1,1792,128]{2,1,0:T(8,128)(2,1)S(1)} collective-permute-done((bf16[1,1792,128]{2,1,0:T(8,128)(2,1)S(1)}, bf16[1,1792,128]{2,1,0:T(8,128)(2,1)S(1)}, u32[]{:S(2)}, u32[]{:S(2)}) %collective-permute-start.1) | collective-permute-done | bytes 458784 | tf_op jit(solution)/shard_map/ppermute | solution.py:52
  23.3 4.6 %collective-permute-start.9 = (bf16[1,1792,128]{2,1,0:T(8,128)(2,1)S(1)}, bf16[1,1792,128]{2,1,0:T(8,128)(2,1)S(1)}, u32[]{:S(2)}, u32[]{:S(2)}) collective-permute-start(bf16[1,1792,128]{2,1,0:T(8,128)(2,1)S(1)} %collective-permute-done.8), channel_id=1, source_target_pairs={{0,15},{1,0},{2,1},{3,2},{4,3},{5,4},{6,5},{7,6},{8,7},{9,8},{10,9... | collective-permute-start | bytes 1376264 | tf_op jit(solution)/shard_map/ppermute | solution.py:56
  27.9 6.1 %collective-permute-done.2 = bf16[1,1792,128]{2,1,0:T(8,128)(2,1)S(1)} collective-permute-done((bf16[1,1792,128]{2,1,0:T(8,128)(2,1)S(1)}, bf16[1,1792,128]{2,1,0:T(8,128)(2,1)S(1)}, u32[]{:S(2)}, u32[]{:S(2)}) %collective-permute-start.2) | collective-permute-done | bytes 458784 | tf_op jit(solution)/shard_map/ppermute | solution.py:52
  35.0 3.6 %collective-permute-start.10 = (bf16[1,1792,128]{2,1,0:T(8,128)(2,1)S(1)}, bf16[1,1792,128]{2,1,0:T(8,128)(2,1)S(1)}, u32[]{:S(2)}, u32[]{:S(2)}) collective-permute-start(bf16[1,1792,128]{2,1,0:T(8,128)(2,1)S(1)} %collective-permute-done.9), channel_id=1, source_target_pairs={{0,15},{1,0},{2,1},{3,2},{4,3},{5,4},{6,5},{7,6},{8,7},{9,8},{10,9... | collective-permute-start | bytes 1376264 | tf_op jit(solution)/shard_map/ppermute | solution.py:56
  38.6 6.1 %collective-permute-done.3 = bf16[1,1792,128]{2,1,0:T(8,128)(2,1)S(1)} collective-permute-done((bf16[1,1792,128]{2,1,0:T(8,128)(2,1)S(1)}, bf16[1,1792,128]{2,1,0:T(8,128)(2,1)S(1)}, u32[]{:S(2)}, u32[]{:S(2)}) %collective-permute-start.3) | collective-permute-done | bytes 458784 | tf_op jit(solution)/shard_map/ppermute | solution.py:52
  44.7 2.4 %collective-permute-start.4 = (bf16[1,1792,128]{2,1,0:T(8,128)(2,1)S(1)}, bf16[1,1792,128]{2,1,0:T(8,128)(2,1)S(1)}, u32[]{:S(2)}, u32[]{:S(2)}) collective-permute-start(bf16[1,1792,128]{2,1,0:T(8,128)(2,1)S(1)} %collective-permute-done.3), channel_id=1, source_target_pairs={{0,1},{1,2},{2,3},{3,4},{4,5},{5,6},{6,7},{7,8},{8,9},{9,10},{10,1... | collective-permute-start | bytes 1376264 | tf_op jit(solution)/shard_map/ppermute | solution.py:52
  48.6 2.1 %collective-permute-start.11 = (bf16[1,1792,128]{2,1,0:T(8,128)(2,1)S(1)}, bf16[1,1792,128]{2,1,0:T(8,128)(2,1)}, u32[]{:S(2)}, u32[]{:S(2)}) collective-permute-start(bf16[1,1792,128]{2,1,0:T(8,128)(2,1)S(1)} %collective-permute-done.10), channel_id=1, source_target_pairs={{0,15},{1,0},{2,1},{3,2},{4,3},{5,4},{6,5},{7,6},{8,7},{9,8},{10,9... | collective-permute-start | bytes 1376264 | tf_op jit(solution)/shard_map/ppermute | solution.py:56
  50.7 4.7 %collective-permute-done.4 = bf16[1,1792,128]{2,1,0:T(8,128)(2,1)S(1)} collective-permute-done((bf16[1,1792,128]{2,1,0:T(8,128)(2,1)S(1)}, bf16[1,1792,128]{2,1,0:T(8,128)(2,1)S(1)}, u32[]{:S(2)}, u32[]{:S(2)}) %collective-permute-start.4) | collective-permute-done | bytes 458784 | tf_op jit(solution)/shard_map/ppermute | solution.py:52
  55.4 4.5 %collective-permute-start.5 = (bf16[1,1792,128]{2,1,0:T(8,128)(2,1)S(1)}, bf16[1,1792,128]{2,1,0:T(8,128)(2,1)}, u32[]{:S(2)}, u32[]{:S(2)}) collective-permute-start(bf16[1,1792,128]{2,1,0:T(8,128)(2,1)S(1)} %collective-permute-done.4), channel_id=1, source_target_pairs={{0,1},{1,2},{2,3},{3,4},{4,5},{5,6},{6,7},{7,8},{8,9},{9,10},{10,1... | collective-permute-start | bytes 1376264 | tf_op jit(solution)/shard_map/ppermute | solution.py:52
  60.7 6.8 %all-to-all-start = ((s32[16,1,12]{2,1,0:T(1,128)}), s32[16,1,12]{2,1,0:T(1,128)S(1)}, u32[]{:S(2)}, u32[]{:S(2)}) async-start(s32[16,1,12]{2,1,0:T(1,128)} %bitcast.12), calls=%async_computation | async-start | bytes 16384 | tf_op jit(solution)/shard_map/all_to_all | solution.py:42
  68.2 5.7 %all-to-all-done = s32[16,1,12]{2,1,0:T(1,128)S(1)} async-done(((s32[16,1,12]{2,1,0:T(1,128)}), s32[16,1,12]{2,1,0:T(1,128)S(1)}, u32[]{:S(2)}, u32[]{:S(2)}) %all-to-all-start) | async-done | bytes 800 | tf_op jit(solution)/shard_map/all_to_all | solution.py:42
  74.6 10.3 %gather_fusion.1 = bf16[192,128,128]{2,1,0:T(8,128)(2,1)} fusion(bf16[128,128,128]{2,1,0:T(8,128)(2,1)} %param.7, s32[1024]{0:T(1024)S(1)} %get-tuple-element.49), kind=kCustom, calls=%fused_computation.1 | custom fusion | bytes 12583680 | tf_op jit(solution)/shard_map/gather | solution.py:44
  87.9 4.1 %collective-permute-start.13 = (bf16[1,1792,128]{2,1,0:T(8,128)(2,1)}, bf16[1,1792,128]{2,1,0:T(8,128)(2,1)S(1)}, u32[]{:S(2)}, u32[]{:S(2)}) collective-permute-start(bf16[1,1792,128]{2,1,0:T(8,128)(2,1)} %collective-permute-done.12), channel_id=1, source_target_pairs={{0,15},{1,0},{2,1},{3,2},{4,3},{5,4},{6,5},{7,6},{8,7},{9,8},{10,9... | collective-permute-start | bytes 1376264 | tf_op jit(solution)/shard_map/ppermute | solution.py:56
  92.0 6.5 %broadcast_select_fusion = bf16[2,8,12,128,128]{4,3,2,1,0:T(8,128)(2,1)} fusion(bf16[2,8,12,128,128]{4,3,2,1,0:T(8,128)(2,1)} %bitcast.77, pred[2,8,12,128]{3,2,1,0:T(8,128)(4,1)S(1)} %iota_compare_fusion, bf16[2,8,12,128]{3,2,1,0:T(8,128)(2,1)S(1)} %broadcast_in_dim.64), kind=kLoop, calls=%fused_computation.10 | loop fusion | flops 3145728 | bytes 12656640 | tf_op jit(solution)/shard_map/jit(_where)/select_n | solution.py:24
  98.5 4.7 %collective-permute-start.14 = (bf16[1,1792,128]{2,1,0:T(8,128)(2,1)S(1)}, bf16[1,1792,128]{2,1,0:T(8,128)(2,1)S(1)}, u32[]{:S(2)}, u32[]{:S(2)}) collective-permute-start(bf16[1,1792,128]{2,1,0:T(8,128)(2,1)S(1)} %collective-permute-done.13), channel_id=1, source_target_pairs={{0,15},{1,0},{2,1},{3,2},{4,3},{5,4},{6,5},{7,6},{8,7},{9,8},{10,9... | collective-permute-start | bytes 1376264 | tf_op jit(solution)/shard_map/ppermute | solution.py:56
  137.3 6.7 %constant_dynamic-slice_fusion = bf16[16,1792,128]{2,1,0:T(8,128)(2,1)} fusion(bf16[32,1792,128]{2,1,0:T(8,128)(2,1)} %constant_dynamic-update-slice_fusion, s32[]{:T(128)S(6)} %select_n.71), kind=kLoop, calls=%fused_computation.76 | loop fusion | bytes 14680068 | tf_op jit(solution)/shard_map/jit(_roll_dynamic)/dynamic_slice | solution.py:59
  144.0 32.9 %while.10 = (s32[]{:T(128)}, f32[2,8,56,12]{2,1,0,3:T(8,128)S(1)}, bf16[2,8,1792,128]{3,2,1,0:T(8,128)(2,1)}, bf16[2,8,12,128,128]{4,3,2,1,0:T(8,128)(2,1)}, s32[]{:T(128)}, /*index=5*/f32[]{:T(128)}) while((s32[]{:T(128)}, f32[2,8,56,12]{2,1,0,3:T(8,128)S(1)}, bf16[2,8,1792,128]{3,2,1,0:T(8,128)(2,1)}, ...), condition=%wide.region_5.6_spmd, body=%wide.region_2.5_spmd.sunk | while | flops 5659164672 | bytes 11065421 | solution.py:65
  144.0 14.4 %convolution_reduce_fusion.2 = f32[8,1792,12]{1,2,0:T(8,128)S(1)} fusion(bf16[2,8,1792,128]{3,2,1,0:T(8,128)(2,1)} %get-tuple-element.89, s32[]{:T(128)} %get-tuple-element.81, bf16[2,8,12,128,128]{4,3,2,1,0:T(8,128)(2,1)} %get-tuple-element.90), kind=kOutput, calls=%fused_computation.3.clone.1 | convolution fusion | flops 5658992640 | bytes 7504896 | tf_op jit(solution)/shard_map/while/body/eval_jaxpr/srd,sgpd->srgp/dot_general | solution.py:11
  160.5 14.4 %convolution_reduce_fusion.2 = f32[8,1792,12]{1,2,0:T(8,128)S(1)} fusion(bf16[2,8,1792,128]{3,2,1,0:T(8,128)(2,1)} %get-tuple-element.89, s32[]{:T(128)} %get-tuple-element.81, bf16[2,8,12,128,128]{4,3,2,1,0:T(8,128)(2,1)} %get-tuple-element.90), kind=kOutput, calls=%fused_computation.3.clone.1 | convolution fusion | flops 5658992640 | bytes 7504896 | tf_op jit(solution)/shard_map/while/body/eval_jaxpr/srd,sgpd->srgp/dot_general | solution.py:11
  177.8 3.5 %all-to-all-start.1 = ((f32[16,1,672]{2,1,0:T(1,128)}), f32[16,1,672]{2,1,0:T(1,128)S(1)}, u32[]{:S(2)}, u32[]{:S(2)}) async-start(f32[16,1,672]{2,1,0:T(1,128)} %reshape.217), calls=%async_computation.1 | async-start | bytes 98304 | tf_op jit(solution)/shard_map/all_to_all | solution.py:69
  181.3 6.7 %all-to-all-done.1 = f32[16,1,672]{2,1,0:T(1,128)S(1)} async-done(((f32[16,1,672]{2,1,0:T(1,128)}), f32[16,1,672]{2,1,0:T(1,128)S(1)}, u32[]{:S(2)}, u32[]{:S(2)}) %all-to-all-start.1) | async-done | bytes 43040 | tf_op jit(solution)/shard_map/all_to_all | solution.py:69
  190.3 3.2 %top_k.9 = (f32[56,128]{1,0:T(8,128)}, s32[56,128]{1,0:T(8,128)}) sort(f32[56,128]{1,0:T(8,128)S(1)} %copy.27, s32[56,128]{1,0:T(8,128)S(1)} %iota.22), dimensions={1}, to_apply=%region_6.7 | sort | flops 93184 | bytes 114688 | tf_op jit(solution)/shard_map/top_k | solution.py:72
  (101 shorter events, 49.4 us)
Async XLA Ops:
  0.6 85.5 %copy-start = (s32[128]{0:T(128)S(1)}, s32[128]{0:T(128)}, u32[]{:S(2)}) copy-start(s32[128]{0:T(128)} %param.8) | copy-start | bytes 1540
  0.6 11.9 %collective-permute-start = (bf16[1,1792,128]{2,1,0:T(8,128)(2,1)}, bf16[1,1792,128]{2,1,0:T(8,128)(2,1)S(1)}, u32[]{:S(2)}, u32[]{:S(2)}) collective-permute-start(bf16[1,1792,128]{2,1,0:T(8,128)(2,1)} %bitcast.79), channel_id=1, source_target_pairs={{0,1},{1,2},{2,3},{3,4},{4,5},{5,6},{6,7},{7,8},{8,9},{9,10},{10,1... | collective-permute-start | bytes 1376264 | tf_op jit(solution)/shard_map/ppermute | solution.py:52
  12.5 10.7 %collective-permute-start.1 = (bf16[1,1792,128]{2,1,0:T(8,128)(2,1)S(1)}, bf16[1,1792,128]{2,1,0:T(8,128)(2,1)S(1)}, u32[]{:S(2)}, u32[]{:S(2)}) collective-permute-start(bf16[1,1792,128]{2,1,0:T(8,128)(2,1)S(1)} %collective-permute-done), channel_id=1, source_target_pairs={{0,1},{1,2},{2,3},{3,4},{4,5},{5,6},{6,7},{7,8},{8,9},{9,10},{10,1... | collective-permute-start | bytes 1376264 | tf_op jit(solution)/shard_map/ppermute | solution.py:52
  12.6 10.8 %collective-permute-start.8 = (bf16[1,1792,128]{2,1,0:T(8,128)(2,1)}, bf16[1,1792,128]{2,1,0:T(8,128)(2,1)S(1)}, u32[]{:S(2)}, u32[]{:S(2)}) collective-permute-start(bf16[1,1792,128]{2,1,0:T(8,128)(2,1)} %bitcast.80), channel_id=1, source_target_pairs={{0,15},{1,0},{2,1},{3,2},{4,3},{5,4},{6,5},{7,6},{8,7},{9,8},{10,9... | collective-permute-start | bytes 1376264 | tf_op jit(solution)/shard_map/ppermute | solution.py:56
  23.3 10.7 %collective-permute-start.2 = (bf16[1,1792,128]{2,1,0:T(8,128)(2,1)S(1)}, bf16[1,1792,128]{2,1,0:T(8,128)(2,1)S(1)}, u32[]{:S(2)}, u32[]{:S(2)}) collective-permute-start(bf16[1,1792,128]{2,1,0:T(8,128)(2,1)S(1)} %collective-permute-done.1), channel_id=1, source_target_pairs={{0,1},{1,2},{2,3},{3,4},{4,5},{5,6},{6,7},{7,8},{8,9},{9,10},{10,1... | collective-permute-start | bytes 1376264 | tf_op jit(solution)/shard_map/ppermute | solution.py:52
  23.3 11.7 %collective-permute-start.9 = (bf16[1,1792,128]{2,1,0:T(8,128)(2,1)S(1)}, bf16[1,1792,128]{2,1,0:T(8,128)(2,1)S(1)}, u32[]{:S(2)}, u32[]{:S(2)}) collective-permute-start(bf16[1,1792,128]{2,1,0:T(8,128)(2,1)S(1)} %collective-permute-done.8), channel_id=1, source_target_pairs={{0,15},{1,0},{2,1},{3,2},{4,3},{5,4},{6,5},{7,6},{8,7},{9,8},{10,9... | collective-permute-start | bytes 1376264 | tf_op jit(solution)/shard_map/ppermute | solution.py:56
  34.0 10.7 %collective-permute-start.3 = (bf16[1,1792,128]{2,1,0:T(8,128)(2,1)S(1)}, bf16[1,1792,128]{2,1,0:T(8,128)(2,1)S(1)}, u32[]{:S(2)}, u32[]{:S(2)}) collective-permute-start(bf16[1,1792,128]{2,1,0:T(8,128)(2,1)S(1)} %collective-permute-done.2), channel_id=1, source_target_pairs={{0,1},{1,2},{2,3},{3,4},{4,5},{5,6},{6,7},{7,8},{8,9},{9,10},{10,1... | collective-permute-start | bytes 1376264 | tf_op jit(solution)/shard_map/ppermute | solution.py:52
  35.0 13.6 %collective-permute-start.10 = (bf16[1,1792,128]{2,1,0:T(8,128)(2,1)S(1)}, bf16[1,1792,128]{2,1,0:T(8,128)(2,1)S(1)}, u32[]{:S(2)}, u32[]{:S(2)}) collective-permute-start(bf16[1,1792,128]{2,1,0:T(8,128)(2,1)S(1)} %collective-permute-done.9), channel_id=1, source_target_pairs={{0,15},{1,0},{2,1},{3,2},{4,3},{5,4},{6,5},{7,6},{8,7},{9,8},{10,9... | collective-permute-start | bytes 1376264 | tf_op jit(solution)/shard_map/ppermute | solution.py:56
  44.7 3.9 %copy-start.2 = (bf16[1,1792,128]{2,1,0:T(8,128)(2,1)}, bf16[1,1792,128]{2,1,0:T(8,128)(2,1)S(1)}, u32[]{:S(2)}) copy-start(bf16[1,1792,128]{2,1,0:T(8,128)(2,1)S(1)} %collective-permute-done.3) | copy-start | bytes 1376260
  44.7 10.7 %collective-permute-start.4 = (bf16[1,1792,128]{2,1,0:T(8,128)(2,1)S(1)}, bf16[1,1792,128]{2,1,0:T(8,128)(2,1)S(1)}, u32[]{:S(2)}, u32[]{:S(2)}) collective-permute-start(bf16[1,1792,128]{2,1,0:T(8,128)(2,1)S(1)} %collective-permute-done.3), channel_id=1, source_target_pairs={{0,1},{1,2},{2,3},{3,4},{4,5},{5,6},{6,7},{7,8},{8,9},{9,10},{10,1... | collective-permute-start | bytes 1376264 | tf_op jit(solution)/shard_map/ppermute | solution.py:52
  48.6 25.4 %collective-permute-start.11 = (bf16[1,1792,128]{2,1,0:T(8,128)(2,1)S(1)}, bf16[1,1792,128]{2,1,0:T(8,128)(2,1)}, u32[]{:S(2)}, u32[]{:S(2)}) collective-permute-start(bf16[1,1792,128]{2,1,0:T(8,128)(2,1)S(1)} %collective-permute-done.10), channel_id=1, source_target_pairs={{0,15},{1,0},{2,1},{3,2},{4,3},{5,4},{6,5},{7,6},{8,7},{9,8},{10,9... | collective-permute-start | bytes 1376264 | tf_op jit(solution)/shard_map/ppermute | solution.py:56
  55.4 19.2 %copy-start.4 = (bf16[1,1792,128]{2,1,0:T(8,128)(2,1)}, bf16[1,1792,128]{2,1,0:T(8,128)(2,1)S(1)}, u32[]{:S(2)}) copy-start(bf16[1,1792,128]{2,1,0:T(8,128)(2,1)S(1)} %collective-permute-done.4) | copy-start | bytes 1376260
  55.4 18.7 %collective-permute-start.5 = (bf16[1,1792,128]{2,1,0:T(8,128)(2,1)S(1)}, bf16[1,1792,128]{2,1,0:T(8,128)(2,1)}, u32[]{:S(2)}, u32[]{:S(2)}) collective-permute-start(bf16[1,1792,128]{2,1,0:T(8,128)(2,1)S(1)} %collective-permute-done.4), channel_id=1, source_target_pairs={{0,1},{1,2},{2,3},{3,4},{4,5},{5,6},{6,7},{7,8},{8,9},{9,10},{10,1... | collective-permute-start | bytes 1376264 | tf_op jit(solution)/shard_map/ppermute | solution.py:52
  60.7 13.2 %all-to-all-start = ((s32[16,1,12]{2,1,0:T(1,128)}), s32[16,1,12]{2,1,0:T(1,128)S(1)}, u32[]{:S(2)}, u32[]{:S(2)}) async-start(s32[16,1,12]{2,1,0:T(1,128)} %bitcast.12), calls=%async_computation | async-start | bytes 16384 | tf_op jit(solution)/shard_map/all_to_all | solution.py:42
  74.0 13.9 %collective-permute-start.12 = (bf16[1,1792,128]{2,1,0:T(8,128)(2,1)}, bf16[1,1792,128]{2,1,0:T(8,128)(2,1)}, u32[]{:S(2)}, u32[]{:S(2)}) collective-permute-start(bf16[1,1792,128]{2,1,0:T(8,128)(2,1)} %collective-permute-done.11), channel_id=1, source_target_pairs={{0,15},{1,0},{2,1},{3,2},{4,3},{5,4},{6,5},{7,6},{8,7},{9,8},{10,9... | collective-permute-start | bytes 1376264 | tf_op jit(solution)/shard_map/ppermute | solution.py:56
  74.1 17.9 %collective-permute-start.6 = (bf16[1,1792,128]{2,1,0:T(8,128)(2,1)}, bf16[1,1792,128]{2,1,0:T(8,128)(2,1)}, u32[]{:S(2)}, u32[]{:S(2)}) collective-permute-start(bf16[1,1792,128]{2,1,0:T(8,128)(2,1)} %collective-permute-done.5), channel_id=1, source_target_pairs={{0,1},{1,2},{2,3},{3,4},{4,5},{5,6},{6,7},{7,8},{8,9},{9,10},{10,1... | collective-permute-start | bytes 1376264 | tf_op jit(solution)/shard_map/ppermute | solution.py:52
  74.6 37.2 %copy-start.1 = (bf16[56,32,128]{2,1,0:T(8,128)(2,1)S(1)}, bf16[56,32,128]{2,1,0:T(8,128)(2,1)}, u32[]{:S(2)}) copy-start(bf16[56,32,128]{2,1,0:T(8,128)(2,1)} %param.6) | copy-start | bytes 1376260
  87.8 19.9 %copy-start.5 = (bf16[1,1792,128]{2,1,0:T(8,128)(2,1)S(1)}, bf16[1,1792,128]{2,1,0:T(8,128)(2,1)}, u32[]{:S(2)}) copy-start(bf16[1,1792,128]{2,1,0:T(8,128)(2,1)} %copy-done.4) | copy-start | bytes 1376260
  87.8 20.7 %copy-start.3 = (bf16[1,1792,128]{2,1,0:T(8,128)(2,1)S(1)}, bf16[1,1792,128]{2,1,0:T(8,128)(2,1)}, u32[]{:S(2)}) copy-start(bf16[1,1792,128]{2,1,0:T(8,128)(2,1)} %copy-done.2) | copy-start | bytes 1376260
  87.9 10.6 %collective-permute-start.13 = (bf16[1,1792,128]{2,1,0:T(8,128)(2,1)}, bf16[1,1792,128]{2,1,0:T(8,128)(2,1)S(1)}, u32[]{:S(2)}, u32[]{:S(2)}) collective-permute-start(bf16[1,1792,128]{2,1,0:T(8,128)(2,1)} %collective-permute-done.12), channel_id=1, source_target_pairs={{0,15},{1,0},{2,1},{3,2},{4,3},{5,4},{6,5},{7,6},{8,7},{9,8},{10,9... | collective-permute-start | bytes 1376264 | tf_op jit(solution)/shard_map/ppermute | solution.py:56
  92.0 11.2 %collective-permute-start.7 = (bf16[1,1792,128]{2,1,0:T(8,128)(2,1)}, bf16[1,1792,128]{2,1,0:T(8,128)(2,1)S(1)}, u32[]{:S(2)}, u32[]{:S(2)}) collective-permute-start(bf16[1,1792,128]{2,1,0:T(8,128)(2,1)} %collective-permute-done.6), channel_id=1, source_target_pairs={{0,1},{1,2},{2,3},{3,4},{4,5},{5,6},{6,7},{7,8},{8,9},{9,10},{10,1... | collective-permute-start | bytes 1376264 | tf_op jit(solution)/shard_map/ppermute | solution.py:52
  98.5 20.9 %collective-permute-start.14 = (bf16[1,1792,128]{2,1,0:T(8,128)(2,1)S(1)}, bf16[1,1792,128]{2,1,0:T(8,128)(2,1)S(1)}, u32[]{:S(2)}, u32[]{:S(2)}) collective-permute-start(bf16[1,1792,128]{2,1,0:T(8,128)(2,1)S(1)} %collective-permute-done.13), channel_id=1, source_target_pairs={{0,15},{1,0},{2,1},{3,2},{4,3},{5,4},{6,5},{7,6},{8,7},{9,8},{10,9... | collective-permute-start | bytes 1376264 | tf_op jit(solution)/shard_map/ppermute | solution.py:56
  144.0 37.3 %copy-start.7 = (s32[1,128]{1,0:T(1,128)S(1)}, s32[1,128]{1,0:T(1,128)}, u32[]{:S(2)}) copy-start(s32[1,128]{1,0:T(1,128)} %param.9) | copy-start | bytes 1540
  177.8 10.2 %all-to-all-start.1 = ((f32[16,1,672]{2,1,0:T(1,128)}), f32[16,1,672]{2,1,0:T(1,128)S(1)}, u32[]{:S(2)}, u32[]{:S(2)}) async-start(f32[16,1,672]{2,1,0:T(1,128)} %reshape.217), calls=%async_computation.1 | async-start | bytes 98304 | tf_op jit(solution)/shard_map/all_to_all | solution.py:69
  (1 other events, 3.2 us)
